TPU v7x, 32 devices: a whole 2x2x4 slice. The times are simulated.
32 devices in a mesh: section: 4 (over z), tile: 8 (over y, x, core).
Axes of the slice: x: 2, y: 2, z: 4, core: 2. Of those that a mesh axis runs over, the one named last changes fastest.
Arguments:
- raw_echo: bfloat16 [2, 2048, 8192], P(None, 'tile', 'section'), may hold values from -6 to 6
- footprint: int32 [4, 8, 8], P('section', 'tile'), may hold values from 0 to 255, as said below
- window_start: int32 [4, 256], P('section', 'tile'), may hold values from 0 to 2047
Outputs:
- image: bfloat16 [4, 8, 1024, 2048], P('section', 'tile')
Inputs may be any that keep to these rules, and one draw needn't show every extreme that they name: `footprint`: each list names 8 different pulse blocks; at most 2 of them lie among the 32 blocks k * 32 to (k + 1) * 32 - 1 of one index k of tile, and in every list some index supplies exactly 2.
All inputs are finite; a program needn't handle non-finite values.
Results may differ from a plain program's by a relative error of at most 0.0071.
Values may be sent and summed in bfloat16 or wider, within the bound.
No kernel may reach another device: no remote copies, remote signals or barrier semaphores. Data moves between devices by JAX's collectives and lax.ppermute only.
A program may use at most 128 MiB of HBM per device.

v0:
```python
import math
import jax
import jax.numpy as jnp
from jax import lax
from jax.sharding import PartitionSpec as P

KC = 128
WIN = 256
PR = 1024
PC = 1024
NP = 8


def passed_along(value, axis, by):
    devices = lax.axis_size(axis)
    pairs = [(i, i + by) for i in range(devices) if 0 <= i + by < devices]
    return lax.ppermute(value, axis, pairs)


def chirp_table(length):
    row_index = lax.broadcasted_iota(jnp.int32, (2 * length, length), 0)
    col_index = lax.broadcasted_iota(jnp.int32, (2 * length, length), 1)
    lag_count = row_index - col_index
    inside = (lag_count >= 0) & (lag_count < length)
    lag_safe = jnp.where(inside, lag_count, 0)
    turn_count = (lag_safe * lag_safe % (2 * length)).astype(jnp.float32)
    phase_angle = turn_count * jnp.float32(math.pi / length)
    scaling = jnp.float32(1.0 / math.sqrt(length))
    real_part = jnp.where(inside, jnp.cos(phase_angle) * scaling, jnp.float32(0.0))
    imag_part = jnp.where(inside, jnp.sin(phase_angle) * scaling, jnp.float32(0.0))
    return (real_part.astype(jnp.bfloat16), imag_part.astype(jnp.bfloat16))


def compress(raw_part, length, keep):
    real_tab, imag_tab = chirp_table(length)
    pulses = raw_part.shape[1]
    blocks = keep // length
    pieces = raw_part.reshape(2, pulses, blocks + 1, length)
    paired = jnp.concatenate([pieces[:, :, :-1], pieces[:, :, 1:]], axis=3).reshape(
        2, pulses * blocks, 2 * length
    )
    real_in = paired[0]
    imag_in = paired[1]
    out_real = jnp.dot(real_in, real_tab, preferred_element_type=jnp.float32) + jnp.dot(
        imag_in, imag_tab, preferred_element_type=jnp.float32
    )
    out_imag = jnp.dot(imag_in, real_tab, preferred_element_type=jnp.float32) - jnp.dot(
        real_in, imag_tab, preferred_element_type=jnp.float32
    )
    stacked = jnp.stack([out_real, out_imag]).reshape(2, pulses, keep)
    return stacked.astype(jnp.bfloat16)


def interp_table(pixel_rows, window_bins):
    upsample = pixel_rows // window_bins
    row_index = lax.broadcasted_iota(jnp.float32, (pixel_rows, window_bins), 0)
    bin_index = lax.broadcasted_iota(jnp.float32, (pixel_rows, window_bins), 1)
    centre = (row_index + 0.5) / upsample - 0.5
    offset = bin_index - centre
    tapering = jnp.cos(offset * (math.pi / 8.0)) ** 2
    kernel = jnp.where(jnp.abs(offset) < 4.0, jnp.sinc(offset) * tapering, 0.0)
    return kernel.astype(jnp.bfloat16)


def tile_image(chosen, block_ids, row_pos, col_pos, interp, pixel_cols):
    entries = chosen.shape[0]
    per_block = chosen.shape[1]
    window_bins = chosen.shape[3]
    merged = chosen.reshape(entries * per_block, 2 * window_bins)
    pulse_ids = (
        block_ids[:, None] * per_block + jnp.arange(per_block, dtype=jnp.int32)[None, :]
    ).reshape(-1)
    columns = col_pos * pixel_cols + jnp.arange(pixel_cols, dtype=jnp.int32) + 1 + 7 * row_pos
    scrambled = columns * 40503 % 65521
    residue = pulse_ids[:, None] * scrambled[None, :] % 65521
    phase_angle = residue.astype(jnp.float32) * jnp.float32(2.0 * math.pi / 65521.0)
    steer_real = jnp.cos(phase_angle).astype(jnp.bfloat16)
    steer_imag = jnp.sin(phase_angle).astype(jnp.bfloat16)
    contract = (((0,), (0,)), ((), ()))
    with_real = lax.dot_general(merged, steer_real, contract, preferred_element_type=jnp.float32)
    with_imag = lax.dot_general(merged, steer_imag, contract, preferred_element_type=jnp.float32)
    scaling = jnp.float32(1.0 / math.sqrt(entries * per_block))
    focus_real = (with_real[:window_bins] - with_imag[window_bins:]) * scaling
    focus_imag = (with_imag[:window_bins] + with_real[window_bins:]) * scaling
    focused = jnp.concatenate([focus_real, focus_imag], axis=1).astype(jnp.bfloat16)
    return jnp.dot(interp, focused, preferred_element_type=jnp.float32).astype(jnp.bfloat16)


def cut_windows(extended, starts, per_block):
    pulses = extended.shape[1]
    span_bins = extended.shape[2]
    grouped = jnp.transpose(
        extended.reshape(2, pulses // per_block, per_block, span_bins), (1, 2, 0, 3)
    )

    def one_block(block_data, start):
        return lax.dynamic_slice_in_dim(block_data, start, WIN, 2)

    return jax.vmap(one_block)(grouped, starts)


def local(raw_echo, footprint, window_start):
    bin_count = raw_echo.shape[2]
    next_rim = passed_along(raw_echo[:, :, :KC], "section", -1)
    own_part = compress(jnp.concatenate([raw_echo, next_rim], axis=2), KC, bin_count)
    next_bins = passed_along(own_part[:, :, :WIN], "section", -1)
    extended = jnp.concatenate([own_part, next_bins], axis=2)
    windows = cut_windows(extended, window_start[0], NP)
    my_list = footprint[0, 0]
    tile_pos = lax.axis_index("tile")
    row_pos = lax.axis_index("section")
    all_blocks = lax.all_gather(windows, "tile", axis=0, tiled=True)
    chosen = jnp.take(all_blocks, my_list, axis=0)
    interp = interp_table(PR, WIN)
    image = tile_image(chosen, my_list, row_pos, tile_pos, interp, PC)
    return image[None, None]


def solution(mesh):
    in_specs = (P(None, "tile", "section"), P("section", "tile", None), P("section", "tile"))
    out_specs = P("section", "tile", None, None)
    return jax.shard_map(local, mesh=mesh, in_specs=in_specs, out_specs=out_specs, check_vma=False)
```

profile of v0, /device:TPU:0, one launch (start us, length us, event | category | flops | bytes accessed | tf_op | source)
XLA Modules:
  0.0 181.1 jit_solution(12100500757804425028)
XLA Ops:
  6.5 0.0 all-gather.2.cloned.1.call-start
  6.5 2.8 %copy.15 = bf16[2,256,2048]{1,2,0:T(8,128)(2,1)S(1)} copy(bf16[2,256,2048]{2,1,0:T(8,128)(2,1)} %param.3) | data formatting | bytes 4194304 | tf_op args[0]
  9.4 1.3 collective-permute-start
  10.7 7.1 %collective-permute-done = bf16[2,256,128]{1,2,0:T(8,128)(2,1)S(1)} collective-permute-done((bf16[2,256,128]{1,2,0:T(8,128)(2,1)S(1)}, bf16[2,256,128]{1,2,0:T(8,128)(2,1)S(1)}, u32[]{:S(2)}, u32[]{:S(2)}) %collective-permute-start) | collective-permute-done | bytes 131104 | tf_op jit(solution)/shard_map/ppermute | solution.py:17
  17.8 0.1 pad_maximum_fusion
  18.0 0.5 fusion.123
  18.5 2.3 %pad_maximum_fusion.1 = (bf16[1,256,16,256]{1,3,2,0:T(8,128)(2,1)}, bf16[1,256,16,256]{1,3,2,0:T(8,128)(2,1)}) fusion(bf16[2,256,16,128]{1,3,2,0:T(8,128)(2,1)S(1)} %get-tuple-element.9, bf16[2,256,16,128]{1,3,2,0:T(8,128)(2,1)S(1)} %get-tuple-element.10), kind=kLoop, calls=%fused_computation.12 | loop fusion | flops 8388608 | bytes 8388608 | tf_op jit(solution)/shard_map/concatenate | solution.py:39
  20.8 3.3 %copy.17 = bf16[1,256,16,256]{3,2,1,0:T(8,128)(2,1)S(1)} copy(bf16[1,256,16,256]{1,3,2,0:T(8,128)(2,1)} %get-tuple-element.7) | data formatting | bytes 4194304 | tf_op jit(solution)/shard_map/slice | solution.py:43
  24.1 2.5 %fusion.63 = f32[4096,128]{1,0:T(8,128)} fusion(bf16[4096,256]{1,0:T(8,128)(2,1)S(1)} %bitcast.27), kind=kOutput, calls=%fused_computation.95 | convolution fusion | flops 269156352 | bytes 4194304 | tf_op jit(solution)/shard_map/dot_general | solution.py:47
  26.6 4.5 %copy.16 = bf16[1,256,16,256]{3,2,1,0:T(8,128)(2,1)} copy(bf16[1,256,16,256]{1,3,2,0:T(8,128)(2,1)} %get-tuple-element.8) | data formatting | bytes 4194304 | tf_op jit(solution)/shard_map/slice | solution.py:42
  31.1 0.0 copy-start
  31.1 0.0 copy-start.1
  31.1 4.2 %fusion.64 = f32[4096,128]{1,0:T(8,128)} fusion(bf16[4096,256]{1,0:T(8,128)(2,1)} %bitcast.29), kind=kOutput, calls=%fused_computation.96 | convolution fusion | flops 269156352 | bytes 4194304 | tf_op jit(solution)/shard_map/dot_general | solution.py:44
  35.4 0.0 copy-done
  35.4 0.0 copy-done.1
  35.4 1.2 fusion.1
  36.6 1.3 stack.10
  37.9 2.8 %fusion = bf16[4096,128]{1,0:T(8,128)(2,1)S(1)} fusion(f32[4096,128]{1,0:T(8,128)} %fusion.64, bf16[4096,256]{1,0:T(8,128)(2,1)S(1)} %bitcast.28), kind=kOutput, calls=%fused_computation.4 | convolution fusion | flops 270204928 | bytes 5242880 | tf_op jit(solution)/shard_map/dot_general | solution.py:44
  40.7 0.0 copy-start.2
  40.7 0.5 stack.9
  41.2 0.0 copy-start.3
  41.2 0.1 constant_dynamic-update-slice_fusion.1
  41.3 0.6 copy-done.2
  41.9 0.1 constant_dynamic-update-slice_fusion
  42.0 1.5 collective-permute-start.1
  43.5 0.0 copy-done.3
  43.5 7.9 %collective-permute-done.1 = bf16[2,256,256]{2,1,0:T(8,128)(2,1)S(1)} collective-permute-done((bf16[2,256,256]{2,1,0:T(8,128)(2,1)S(1)}, bf16[2,256,256]{2,1,0:T(8,128)(2,1)S(1)}, u32[]{:S(2)}, u32[]{:S(2)}) %collective-permute-start.1) | collective-permute-done | bytes 262176 | tf_op jit(solution)/shard_map/ppermute | solution.py:17
  51.4 0.2 maximum_bitcast_fusion
  51.6 60.6 %copy.18 = bf16[2,32,8,2304]{2,0,1,3:T(2,128)(2,1)} copy(bf16[2,32,8,2304]{3,2,1,0:T(8,128)(2,1)S(1)} %maximum_bitcast_fusion) | data formatting | bytes 4718592 | tf_op jit(solution)/shard_map/reshape | solution.py:93
  112.2 11.5 %gather_fusion.1 = bf16[32,8,2,256]{1,2,3,0:T(2,128)(2,1)} fusion(bf16[32,8,2,2304]{1,2,0,3:T(2,128)(2,1)} %bitcast.26, s32[32]{0:T(128)S(1)} %fusion.72), kind=kCustom, calls=%fused_computation.1 | custom fusion | bytes 524800 | tf_op jit(solution)/shard_map/vmap()/gather | solution.py:97
  123.8 0.0 copy-start.4
  123.8 9.2 %copy.19 = bf16[32,8,2,256]{3,1,2,0:T(8,128)(2,1)} copy(bf16[32,8,2,256]{1,2,3,0:T(2,128)(2,1)} %gather_fusion.1) | data formatting | bytes 524288 | tf_op jit(solution)/shard_map/vmap()/gather | solution.py:97
  133.0 0.0 all-gather.2.cloned.1.call-update
  133.0 0.0 copy-done.4
  133.0 0.1 iota_add_fusion
  133.1 0.1 add.195
  133.2 0.1 broadcast_in_dim.34
  133.3 0.1 broadcast_in_dim.35
  133.4 27.7 %all-gather.2.cloned.1.call-done = bf16[256,8,2,256]{3,1,2,0:T(8,128)(2,1)} async-done(((bf16[32,8,2,256]{3,1,2,0:T(8,128)(2,1)}), bf16[256,8,2,256]{3,1,2,0:T(8,128)(2,1)}) %all-gather.2.cloned.1.call-update) | async-done | bytes 2097168 | tf_op jit(solution)/shard_map/all_gather | solution.py:112
  161.1 2.1 %gather_fusion = bf16[8,8,2,256]{3,1,2,0:T(8,128)(2,1)S(1)} fusion(bf16[256,8,2,256]{3,1,2,0:T(8,128)(2,1)} %all-gather.2.cloned.1.call-done, s32[1024]{0:T(1024)S(1)} %pad_clamp_fusion), kind=kCustom, calls=%fused_computation | custom fusion | bytes 131104 | tf_op jit(solution)/shard_map/jit(_take)/gather | solution.py:113
  163.3 1.4 fusion.48
  164.7 1.4 fusion.49
  166.1 0.5 fusion.14
  166.6 7.6 %convert_bitcast_fusion = bf16[1,1,1024,2048]{3,2,1,0:T(8,128)(2,1)} fusion(bf16[256,1024]{1,0:T(8,128)(2,1)S(1)} %get-tuple-element.6, bf16[256,1024]{1,0:T(8,128)(2,1)S(1)} %get-tuple-element.5, f32[1024]{0:T(1024)S(1)} %multiply_add_fusion.1), kind=kOutput, calls=%fused_computation.8 | convolution fusion | flops 1088421888 | bytes 5246976 | tf_op jit(solution)/shard_map/dot_general | solution.py:86
  (9 shorter events, 0.1 us)
Async XLA Ops:
  6.5 154.6 %all-gather.2.cloned.1.call-start = ((), (), s32[]{:S(2)}) async-start(), calls=%async_computation | async-start | bytes 2359296 | tf_op jit(solution)/shard_map/all_gather | solution.py:112
  9.4 8.4 %collective-permute-start = (bf16[2,256,128]{1,2,0:T(8,128)(2,1)S(1)}, bf16[2,256,128]{1,2,0:T(8,128)(2,1)S(1)}, u32[]{:S(2)}, u32[]{:S(2)}) collective-permute-start(bf16[2,256,128]{1,2,0:T(8,128)(2,1)S(1)} %slice.51), channel_id=1, source_target_pairs={{8,0},{16,8},{24,16},{9,1},{17,9},{25,17},{10,2},{18,10},{26,18},{... | collective-permute-start | bytes 393224 | tf_op jit(solution)/shard_map/ppermute | solution.py:17
  31.1 4.3 %copy-start = (bf16[1,256,16,256]{3,2,1,0:T(8,128)(2,1)S(1)}, bf16[1,256,16,256]{3,2,1,0:T(8,128)(2,1)}, u32[]{:S(2)}) copy-start(bf16[1,256,16,256]{3,2,1,0:T(8,128)(2,1)} %copy.16) | copy-start | bytes 6291460
  31.1 4.3 %copy-start.1 = (f32[4096,128]{1,0:T(8,128)S(1)}, f32[4096,128]{1,0:T(8,128)}, u32[]{:S(2)}) copy-start(f32[4096,128]{1,0:T(8,128)} %fusion.63) | copy-start | bytes 6291460
  40.7 1.2 copy-start.2
  41.2 2.3 %copy-start.3 = (s32[1,32]{1,0:T(1,128)S(1)}, s32[1,32]{1,0:T(1,128)}, u32[]{:S(2)}) copy-start(s32[1,32]{1,0:T(1,128)} %param.5) | copy-start | bytes 388
  42.0 9.4 %collective-permute-start.1 = (bf16[2,256,256]{2,1,0:T(8,128)(2,1)S(1)}, bf16[2,256,256]{2,1,0:T(8,128)(2,1)S(1)}, u32[]{:S(2)}, u32[]{:S(2)}) collective-permute-start(bf16[2,256,256]{2,1,0:T(8,128)(2,1)S(1)} %slice.56), channel_id=1, source_target_pairs={{8,0},{16,8},{24,16},{9,1},{17,9},{25,17},{10,2},{18,10},{26,18},{... | collective-permute-start | bytes 786440 | tf_op jit(solution)/shard_map/ppermute | solution.py:17
  123.8 9.2 %copy-start.4 = (s32[1,1,8]{2,1,0:T(1,128)S(1)}, s32[1,1,8]{2,1,0:T(1,128)}, u32[]{:S(2)}) copy-start(s32[1,1,8]{2,1,0:T(1,128)} %param.4) | copy-start | bytes 100
Sparse Core Ops, SparseCore 0:
  133.1 27.9 all-gather.1
where the time goes:
time: 182 us; the launch traced here: 181 us
  local copies, waits for them, and re-layouts  97.6 us (54%)
  waiting for transfers between devices  42.7 us (23%)
  matrix products  21.3 us (12%)
  between operations  13.6 us (7%)
  other arithmetic  3.22 us (2%)
  starting transfers between devices  2.77 us (2%)
    reshape x1, local copies, waits for them, and re-layouts, cut_windows(): extended.reshape(2, pulses // per_block, per_block, span_bins)  60.6 us
    all_gather x1, waiting for transfers between devices, local(): all_blocks = lax.all_gather(windows, 'tile', axis=0, tiled=True)  27.7 us
    gather x2, local copies, waits for them, and re-layouts, one_block(): return lax.dynamic_slice_in_dim(block_data, start, WIN, 2)  20.7 us
    ppermute x2, waiting for transfers between devices, passed_along(): return lax.ppermute(value, axis, pairs)  15 us
    dot_general x1, matrix products, tile_image(): jnp.dot(interp, focused, preferred_element_type=jnp.float32)  7.65 us
    slice x1, local copies, waits for them, and re-layouts, compress(): real_in = paired[0]  4.49 us
    dot_general x1, matrix products, compress(): jnp.dot(real_in, real_tab, preferred_element_type=jnp.float32)  4.25 us
  transfers between devices with their start and end apart: 3, of which 3 were waited for; matrix products, arithmetic and copies ran while one was open for 0% of the time, Pallas kernels for 0%

commit v1 on v0

--- a/solution.py
+++ b/solution.py
@@ -1,14 +1,35 @@
+import functools
 import math
 import jax
 import jax.numpy as jnp
 from jax import lax
 from jax.sharding import PartitionSpec as P
+from jax.lax import axis_index, axis_size, ppermute
 
 KC = 128
 WIN = 256
 PR = 1024
 PC = 1024
 NP = 8
+
+
+def reach_gates(row_data, pos_dim):
+    earlier, finding, oldest = (axis_size("tile"), axis_index("tile"), row_data.shape[pos_dim])
+    slots = [pp * earlier if b == pos_dim else pp for b, pp in enumerate(row_data.shape)]
+    e_now = lax.dynamic_update_slice_in_dim(
+        jnp.zeros(slots, row_data.dtype), row_data, finding * oldest, axis=pos_dim
+    )
+    for p in tuple(range(1, earlier)):
+        row_data = ppermute(
+            row_data, axis_name="tile", perm=[(b, (b + 1) % earlier) for b in range(earlier)]
+        )
+        e_now = lax.dynamic_update_slice_in_dim(
+            e_now, row_data, (finding - p) % earlier * oldest, axis=pos_dim
+        )
+    return e_now
+
+
+rest_series_over_axis = functools.partial(reach_gates, pos_dim=0)
 
 
 def passed_along(value, axis, by):
@@ -109,7 +130,7 @@
     my_list = footprint[0, 0]
     tile_pos = lax.axis_index("tile")
     row_pos = lax.axis_index("section")
-    all_blocks = lax.all_gather(windows, "tile", axis=0, tiled=True)
+    all_blocks = rest_series_over_axis(windows)
     chosen = jnp.take(all_blocks, my_list, axis=0)
     interp = interp_table(PR, WIN)
     image = tile_image(chosen, my_list, row_pos, tile_pos, interp, PC)

time: 182 us -> 185 us (1.016)
  waiting for transfers between devices: 42.7 us -> 60.5 us
  between operations: 13.6 us -> 0.4 us
    ppermute x0 -> x7, waiting for transfers between devices: none -> 45.3 us  [reach_gates(): ppermute(row_data, axis_name='tile', perm=[(b, (b + 1) % earlier) for b i...]
    all_gather x1 -> x0, waiting for transfers between devices: 27.7 us -> none  [local(): all_blocks = lax.all_gather(windows, 'tile', axis=0, tiled=True)]
  transfers between devices with their start and end apart: 3 -> 9, of which waited for: 3 -> 9; matrix products, arithmetic and copies ran while one was open for 0% -> 1% of each run, Pallas kernels for 0% -> 0%
where the time goes in v1:
time: 185 us; the launch traced here: 184 us
  local copies, waits for them, and re-layouts  96.2 us (52%)
  waiting for transfers between devices  60.5 us (33%)
  matrix products  21.3 us (12%)
  other arithmetic  3.23 us (2%)
  starting transfers between devices  2.66 us (1%)
    reshape x1, local copies, waits for them, and re-layouts, cut_windows(): extended.reshape(2, pulses // per_block, per_block, span_bins)  60.7 us
    ppermute x7, waiting for transfers between devices, reach_gates(): ppermute(row_data, axis_name='tile', perm=[(b, (b + 1) % earlier) for b i...  45.3 us
    gather x2, local copies, waits for them, and re-layouts, one_block(): return lax.dynamic_slice_in_dim(block_data, start, WIN, 2)  19.7 us
    ppermute x2, waiting for transfers between devices, passed_along(): return lax.ppermute(value, axis, pairs)  15.2 us
    dot_general x1, matrix products, tile_image(): jnp.dot(interp, focused, preferred_element_type=jnp.float32)  7.65 us
    slice x1, local copies, waits for them, and re-layouts, compress(): real_in = paired[0]  4.49 us
    dot_general x1, matrix products, compress(): jnp.dot(real_in, real_tab, preferred_element_type=jnp.float32)  4.27 us
  transfers between devices with their start and end apart: 9, of which 9 were waited for; matrix products, arithmetic and copies ran while one was open for 1% of the time, Pallas kernels for 0%

profile of v1, /device:TPU:0, one launch (start us, length us, event | category | flops | bytes accessed | tf_op | source)
XLA Modules:
  0.0 184.3 jit_solution(6999003186506012455)
XLA Ops:
  0.0 2.8 %copy.21 = bf16[2,256,2048]{1,2,0:T(8,128)(2,1)S(1)} copy(bf16[2,256,2048]{2,1,0:T(8,128)(2,1)} %param.3) | data formatting | bytes 4194304 | tf_op args[0]
  2.9 1.3 collective-permute-start
  4.2 7.1 %collective-permute-done = bf16[2,256,128]{1,2,0:T(8,128)(2,1)S(1)} collective-permute-done((bf16[2,256,128]{1,2,0:T(8,128)(2,1)S(1)}, bf16[2,256,128]{1,2,0:T(8,128)(2,1)S(1)}, u32[]{:S(2)}, u32[]{:S(2)}) %collective-permute-start) | collective-permute-done | bytes 131104 | tf_op jit(solution)/shard_map/ppermute | solution.py:38
  11.3 0.1 pad_maximum_fusion
  11.4 0.5 fusion.123
  12.0 2.3 %pad_maximum_fusion.1 = (bf16[1,256,16,256]{1,3,2,0:T(8,128)(2,1)}, bf16[1,256,16,256]{1,3,2,0:T(8,128)(2,1)}) fusion(bf16[2,256,16,128]{1,3,2,0:T(8,128)(2,1)S(1)} %get-tuple-element.9, bf16[2,256,16,128]{1,3,2,0:T(8,128)(2,1)S(1)} %get-tuple-element.10), kind=kLoop, calls=%fused_computation.12 | loop fusion | flops 8388608 | bytes 8388608 | tf_op jit(solution)/shard_map/concatenate | solution.py:60
  14.2 3.3 %copy.23 = bf16[1,256,16,256]{3,2,1,0:T(8,128)(2,1)S(1)} copy(bf16[1,256,16,256]{1,3,2,0:T(8,128)(2,1)} %get-tuple-element.7) | data formatting | bytes 4194304 | tf_op jit(solution)/shard_map/slice | solution.py:64
  17.6 2.5 %fusion.63 = f32[4096,128]{1,0:T(8,128)} fusion(bf16[4096,256]{1,0:T(8,128)(2,1)S(1)} %bitcast.27), kind=kOutput, calls=%fused_computation.95 | convolution fusion | flops 269156352 | bytes 4194304 | tf_op jit(solution)/shard_map/dot_general | solution.py:68
  20.1 4.5 %copy.22 = bf16[1,256,16,256]{3,2,1,0:T(8,128)(2,1)} copy(bf16[1,256,16,256]{1,3,2,0:T(8,128)(2,1)} %get-tuple-element.8) | data formatting | bytes 4194304 | tf_op jit(solution)/shard_map/slice | solution.py:63
  24.6 0.0 copy-start
  24.6 0.0 copy-start.1
  24.6 4.3 %fusion.64 = f32[4096,128]{1,0:T(8,128)} fusion(bf16[4096,256]{1,0:T(8,128)(2,1)} %bitcast.29), kind=kOutput, calls=%fused_computation.96 | convolution fusion | flops 269156352 | bytes 4194304 | tf_op jit(solution)/shard_map/dot_general | solution.py:65
  28.9 0.0 copy-done
  28.9 0.0 copy-done.1
  28.9 1.2 fusion.1
  30.1 1.3 stack.10
  31.4 2.8 %fusion = bf16[4096,128]{1,0:T(8,128)(2,1)S(1)} fusion(f32[4096,128]{1,0:T(8,128)} %fusion.64, bf16[4096,256]{1,0:T(8,128)(2,1)S(1)} %bitcast.28), kind=kOutput, calls=%fused_computation.4 | convolution fusion | flops 270204928 | bytes 5242880 | tf_op jit(solution)/shard_map/dot_general | solution.py:65
  34.2 0.0 copy-start.2
  34.2 0.5 stack.9
  34.7 0.0 copy-start.3
  34.7 0.1 constant_dynamic-update-slice_fusion.1
  34.8 0.6 copy-done.2
  35.4 0.1 constant_dynamic-update-slice_fusion
  35.5 1.3 collective-permute-start.1
  36.8 0.0 copy-done.3
  36.8 8.1 %collective-permute-done.1 = bf16[2,256,256]{2,1,0:T(8,128)(2,1)S(1)} collective-permute-done((bf16[2,256,256]{2,1,0:T(8,128)(2,1)S(1)}, bf16[2,256,256]{2,1,0:T(8,128)(2,1)S(1)}, u32[]{:S(2)}, u32[]{:S(2)}) %collective-permute-start.1) | collective-permute-done | bytes 262176 | tf_op jit(solution)/shard_map/ppermute | solution.py:38
  44.9 0.2 maximum_bitcast_fusion
  45.1 60.7 %copy.24 = bf16[2,32,8,2304]{2,0,1,3:T(2,128)(2,1)} copy(bf16[2,32,8,2304]{3,2,1,0:T(8,128)(2,1)S(1)} %maximum_bitcast_fusion) | data formatting | bytes 4718592 | tf_op jit(solution)/shard_map/reshape | solution.py:114
  105.8 11.5 %gather_fusion.1 = bf16[32,8,2,256]{1,2,3,0:T(2,128)(2,1)} fusion(bf16[32,8,2,2304]{1,2,0,3:T(2,128)(2,1)} %bitcast.26, s32[32]{0:T(128)S(1)} %fusion.78), kind=kCustom, calls=%fused_computation.1 | custom fusion | bytes 524800 | tf_op jit(solution)/shard_map/vmap()/gather | solution.py:118
  117.3 0.0 copy-start.4
  117.3 8.1 %copy.25 = bf16[32,8,2,256]{3,1,2,0:T(8,128)(2,1)S(1)} copy(bf16[32,8,2,256]{1,2,3,0:T(2,128)(2,1)} %gather_fusion.1) | data formatting | bytes 524288 | tf_op jit(solution)/shard_map/vmap()/gather | solution.py:118
  125.5 0.1 collective-permute-start.2
  125.6 6.7 %collective-permute-done.2 = bf16[32,8,2,256]{3,1,2,0:T(8,128)(2,1)S(1)} collective-permute-done((bf16[32,8,2,256]{3,1,2,0:T(8,128)(2,1)S(1)}, bf16[32,8,2,256]{3,1,2,0:T(8,128)(2,1)S(1)}, u32[]{:S(2)}, u32[]{:S(2)}) %collective-permute-start.2) | collective-permute-done | bytes 262176 | tf_op jit(solution)/shard_map/ppermute | solution.py:23
  132.2 0.0 collective-permute-start.3
  132.2 0.0 copy-done.4
  132.2 6.7 %collective-permute-done.3 = bf16[32,8,2,256]{3,1,2,0:T(8,128)(2,1)S(1)} collective-permute-done((bf16[32,8,2,256]{3,1,2,0:T(8,128)(2,1)S(1)}, bf16[32,8,2,256]{3,1,2,0:T(8,128)(2,1)S(1)}, u32[]{:S(2)}, u32[]{:S(2)}) %collective-permute-start.3) | collective-permute-done | bytes 262176 | tf_op jit(solution)/shard_map/ppermute | solution.py:23
  138.9 0.0 collective-permute-start.4
  138.9 6.7 %collective-permute-done.4 = bf16[32,8,2,256]{3,1,2,0:T(8,128)(2,1)S(1)} collective-permute-done((bf16[32,8,2,256]{3,1,2,0:T(8,128)(2,1)S(1)}, bf16[32,8,2,256]{3,1,2,0:T(8,128)(2,1)S(1)}, u32[]{:S(2)}, u32[]{:S(2)}) %collective-permute-start.4) | collective-permute-done | bytes 262176 | tf_op jit(solution)/shard_map/ppermute | solution.py:23
  145.6 0.0 collective-permute-start.5
  145.6 0.1 iota_add_fusion
  145.7 6.6 %collective-permute-done.5 = bf16[32,8,2,256]{3,1,2,0:T(8,128)(2,1)S(1)} collective-permute-done((bf16[32,8,2,256]{3,1,2,0:T(8,128)(2,1)S(1)}, bf16[32,8,2,256]{3,1,2,0:T(8,128)(2,1)S(1)}, u32[]{:S(2)}, u32[]{:S(2)}) %collective-permute-start.5) | collective-permute-done | bytes 262176 | tf_op jit(solution)/shard_map/ppermute | solution.py:23
  152.3 0.0 collective-permute-start.6
  152.5 0.1 add.263
  152.6 0.1 broadcast_in_dim.37
  152.6 0.1 broadcast_in_dim.38
  152.8 0.1 broadcast_in_dim.40
  152.9 6.2 %collective-permute-done.6 = bf16[32,8,2,256]{3,1,2,0:T(8,128)(2,1)} collective-permute-done((bf16[32,8,2,256]{3,1,2,0:T(8,128)(2,1)S(1)}, bf16[32,8,2,256]{3,1,2,0:T(8,128)(2,1)}, u32[]{:S(2)}, u32[]{:S(2)}) %collective-permute-start.6) | collective-permute-done | bytes 262176 | tf_op jit(solution)/shard_map/ppermute | solution.py:23
  159.1 0.0 collective-permute-start.7
  159.2 6.8 %collective-permute-done.7 = bf16[32,8,2,256]{3,1,2,0:T(8,128)(2,1)S(1)} collective-permute-done((bf16[32,8,2,256]{3,1,2,0:T(8,128)(2,1)}, bf16[32,8,2,256]{3,1,2,0:T(8,128)(2,1)S(1)}, u32[]{:S(2)}, u32[]{:S(2)}) %collective-permute-start.7) | collective-permute-done | bytes 262176 | tf_op jit(solution)/shard_map/ppermute | solution.py:23
  166.0 0.0 collective-permute-start.8
  166.1 1.0 constant_dynamic-update-slice_fusion.4
  167.1 5.7 %collective-permute-done.8 = bf16[32,8,2,256]{3,1,2,0:T(8,128)(2,1)S(1)} collective-permute-done((bf16[32,8,2,256]{3,1,2,0:T(8,128)(2,1)S(1)}, bf16[32,8,2,256]{3,1,2,0:T(8,128)(2,1)S(1)}, u32[]{:S(2)}, u32[]{:S(2)}) %collective-permute-start.8) | collective-permute-done | bytes 262176 | tf_op jit(solution)/shard_map/ppermute | solution.py:23
  172.8 0.6 gather_fusion
  173.3 1.4 fusion.48
  174.7 1.4 fusion.49
  176.1 0.5 fusion.14
  176.7 7.6 %convert_bitcast_fusion = bf16[1,1,1024,2048]{3,2,1,0:T(8,128)(2,1)} fusion(bf16[256,1024]{1,0:T(8,128)(2,1)S(1)} %get-tuple-element.6, bf16[256,1024]{1,0:T(8,128)(2,1)S(1)} %get-tuple-element.5, f32[1024]{0:T(1024)S(1)} %multiply_add_fusion.1), kind=kOutput, calls=%fused_computation.8 | convolution fusion | flops 1088421888 | bytes 5246976 | tf_op jit(solution)/shard_map/dot_general | solution.py:107
  (16 shorter events, 0.3 us)
Async XLA Ops:
  2.9 8.4 %collective-permute-start = (bf16[2,256,128]{1,2,0:T(8,128)(2,1)S(1)}, bf16[2,256,128]{1,2,0:T(8,128)(2,1)S(1)}, u32[]{:S(2)}, u32[]{:S(2)}) collective-permute-start(bf16[2,256,128]{1,2,0:T(8,128)(2,1)S(1)} %slice.51), channel_id=1, source_target_pairs={{8,0},{16,8},{24,16},{9,1},{17,9},{25,17},{10,2},{18,10},{26,18},{... | collective-permute-start | bytes 393224 | tf_op jit(solution)/shard_map/ppermute | solution.py:38
  24.6 4.3 %copy-start = (bf16[1,256,16,256]{3,2,1,0:T(8,128)(2,1)S(1)}, bf16[1,256,16,256]{3,2,1,0:T(8,128)(2,1)}, u32[]{:S(2)}) copy-start(bf16[1,256,16,256]{3,2,1,0:T(8,128)(2,1)} %copy.22) | copy-start | bytes 6291460
  24.6 4.3 %copy-start.1 = (f32[4096,128]{1,0:T(8,128)S(1)}, f32[4096,128]{1,0:T(8,128)}, u32[]{:S(2)}) copy-start(f32[4096,128]{1,0:T(8,128)} %fusion.63) | copy-start | bytes 6291460
  34.2 1.2 copy-start.2
  34.7 2.1 %copy-start.3 = (s32[1,32]{1,0:T(1,128)S(1)}, s32[1,32]{1,0:T(1,128)}, u32[]{:S(2)}) copy-start(s32[1,32]{1,0:T(1,128)} %param.5) | copy-start | bytes 388
  35.5 9.4 %collective-permute-start.1 = (bf16[2,256,256]{2,1,0:T(8,128)(2,1)S(1)}, bf16[2,256,256]{2,1,0:T(8,128)(2,1)S(1)}, u32[]{:S(2)}, u32[]{:S(2)}) collective-permute-start(bf16[2,256,256]{2,1,0:T(8,128)(2,1)S(1)} %slice.56), channel_id=1, source_target_pairs={{8,0},{16,8},{24,16},{9,1},{17,9},{25,17},{10,2},{18,10},{26,18},{... | collective-permute-start | bytes 786440 | tf_op jit(solution)/shard_map/ppermute | solution.py:38
  117.3 14.9 %copy-start.4 = (s32[1,1,8]{2,1,0:T(1,128)S(1)}, s32[1,1,8]{2,1,0:T(1,128)}, u32[]{:S(2)}) copy-start(s32[1,1,8]{2,1,0:T(1,128)} %param.4) | copy-start | bytes 100
  125.5 6.7 %collective-permute-start.2 = (bf16[32,8,2,256]{3,1,2,0:T(8,128)(2,1)S(1)}, bf16[32,8,2,256]{3,1,2,0:T(8,128)(2,1)S(1)}, u32[]{:S(2)}, u32[]{:S(2)}) collective-permute-start(bf16[32,8,2,256]{3,1,2,0:T(8,128)(2,1)S(1)} %copy.25), channel_id=1, source_target_pairs={{0,1},{1,2},{2,3},{3,4},{4,5},{5,6},{6,7},{7,0},{8,9},{9,10},{10,1... | collective-permute-start | bytes 786440 | tf_op jit(solution)/shard_map/ppermute | solution.py:23
  132.2 6.7 %collective-permute-start.3 = (bf16[32,8,2,256]{3,1,2,0:T(8,128)(2,1)S(1)}, bf16[32,8,2,256]{3,1,2,0:T(8,128)(2,1)S(1)}, u32[]{:S(2)}, u32[]{:S(2)}) collective-permute-start(bf16[32,8,2,256]{3,1,2,0:T(8,128)(2,1)S(1)} %collective-permute-done.2), channel_id=1, source_target_pairs={{0,1},{1,2},{2,3},{3,4},{4,5},{5,6},{6,7},{7,0},{8,9},{9,10},{10,1... | collective-permute-start | bytes 786440 | tf_op jit(solution)/shard_map/ppermute | solution.py:23
  138.9 6.7 %collective-permute-start.4 = (bf16[32,8,2,256]{3,1,2,0:T(8,128)(2,1)S(1)}, bf16[32,8,2,256]{3,1,2,0:T(8,128)(2,1)S(1)}, u32[]{:S(2)}, u32[]{:S(2)}) collective-permute-start(bf16[32,8,2,256]{3,1,2,0:T(8,128)(2,1)S(1)} %collective-permute-done.3), channel_id=1, source_target_pairs={{0,1},{1,2},{2,3},{3,4},{4,5},{5,6},{6,7},{7,0},{8,9},{9,10},{10,1... | collective-permute-start | bytes 786440 | tf_op jit(solution)/shard_map/ppermute | solution.py:23
  145.6 6.7 %collective-permute-start.5 = (bf16[32,8,2,256]{3,1,2,0:T(8,128)(2,1)S(1)}, bf16[32,8,2,256]{3,1,2,0:T(8,128)(2,1)S(1)}, u32[]{:S(2)}, u32[]{:S(2)}) collective-permute-start(bf16[32,8,2,256]{3,1,2,0:T(8,128)(2,1)S(1)} %collective-permute-done.4), channel_id=1, source_target_pairs={{0,1},{1,2},{2,3},{3,4},{4,5},{5,6},{6,7},{7,0},{8,9},{9,10},{10,1... | collective-permute-start | bytes 786440 | tf_op jit(solution)/shard_map/ppermute | solution.py:23
  152.3 6.8 %collective-permute-start.6 = (bf16[32,8,2,256]{3,1,2,0:T(8,128)(2,1)S(1)}, bf16[32,8,2,256]{3,1,2,0:T(8,128)(2,1)}, u32[]{:S(2)}, u32[]{:S(2)}) collective-permute-start(bf16[32,8,2,256]{3,1,2,0:T(8,128)(2,1)S(1)} %collective-permute-done.5), channel_id=1, source_target_pairs={{0,1},{1,2},{2,3},{3,4},{4,5},{5,6},{6,7},{7,0},{8,9},{9,10},{10,1... | collective-permute-start | bytes 786440 | tf_op jit(solution)/shard_map/ppermute | solution.py:23
  159.1 6.9 %collective-permute-start.7 = (bf16[32,8,2,256]{3,1,2,0:T(8,128)(2,1)}, bf16[32,8,2,256]{3,1,2,0:T(8,128)(2,1)S(1)}, u32[]{:S(2)}, u32[]{:S(2)}) collective-permute-start(bf16[32,8,2,256]{3,1,2,0:T(8,128)(2,1)} %collective-permute-done.6), channel_id=1, source_target_pairs={{0,1},{1,2},{2,3},{3,4},{4,5},{5,6},{6,7},{7,0},{8,9},{9,10},{10,1... | collective-permute-start | bytes 786440 | tf_op jit(solution)/shard_map/ppermute | solution.py:23
  166.0 6.7 %collective-permute-start.8 = (bf16[32,8,2,256]{3,1,2,0:T(8,128)(2,1)S(1)}, bf16[32,8,2,256]{3,1,2,0:T(8,128)(2,1)S(1)}, u32[]{:S(2)}, u32[]{:S(2)}) collective-permute-start(bf16[32,8,2,256]{3,1,2,0:T(8,128)(2,1)S(1)} %collective-permute-done.7), channel_id=1, source_target_pairs={{0,1},{1,2},{2,3},{3,4},{4,5},{5,6},{6,7},{7,0},{8,9},{9,10},{10,1... | collective-permute-start | bytes 786440 | tf_op jit(solution)/shard_map/ppermute | solution.py:23
